TPU v7x, 32 devices: a whole 2x2x4 slice. The times are simulated.
32 devices in a mesh: region: 2 (over x), var: 8 (over z, y), samp: 2 (over core).
Axes of the slice: x: 2, y: 2, z: 4, core: 2. Of those that a mesh axis runs over, the one named last changes fastest.
Arguments:
- dosage: bfloat16 [2048, 16384], P('samp', ('region', 'var')), parts along dimension 1, may hold values from 0 to 2
- observed: int32 [2048, 16384], P('samp', ('region', 'var')), parts along dimension 1, may hold values from 0 to 1, as said below
- counts: int32 [16], P(('region', 'var')), parts along dimension 0, may hold values from 1 to 4, as said below
Outputs:
- correlations: bfloat16 [16, 4, 1024, 1024], P(('region', 'var'), None, 'samp'), parts along dimension 0
There are 2 independent parts, one for each index of `region`. A program takes and returns all parts, laid end to end along the dimension named above; each array names one. Nothing has to cross between parts.
Inputs may be any that keep to these rules, and one draw needn't show every extreme that they name: Block b's partners are blocks b to b + counts[b] - 1; counts[b] is at most 8 - b, and counts[0] = 4. `observed`: some variants are missing in every sample.
All inputs are finite; a program needn't handle non-finite values.
Results may differ from a plain program's by a relative error of at most 0.001.
The roundings to bfloat16 on the way count: a program that leaves them out, or rounds other values in their place, can miss the bound.
Values may be sent and summed in bfloat16 or wider, within the bound.
A program may use at most 128 MiB of HBM per device.

v0:
```python
import jax
import jax.numpy as jnp
from jax import lax
from jax.sharding import PartitionSpec as P

WIN = 4


epsilon = 1e-05


def from_behind(shard, axis, by):
    count = lax.axis_size(axis)
    pairs = [(i, i + by) for i in range(count) if 0 <= i + by < count]
    return lax.ppermute(shard, axis, pairs)


def contract(left, right):
    return lax.dot_general(
        left, right, (((0,), (0,)), ((), ())), preferred_element_type=jnp.float32
    )


def per_device(dosage, observed, counts):
    values = dosage.astype(jnp.float32)
    present = observed.astype(jnp.float32)
    present_count, summed, squares = lax.psum(
        (
            jnp.sum(present, axis=0),
            jnp.sum(present * values, axis=0),
            jnp.sum(present * values * values, axis=0),
        ),
        "samp",
    )
    present_count = jnp.maximum(present_count, 1.0)
    center = summed / present_count
    offsets = present * (values - center)
    spread = squares / present_count - center * center
    scored = (offsets * lax.rsqrt(spread + epsilon)).astype(jnp.bfloat16)
    width = scored.shape[1]
    total_samples = float(scored.shape[0] * lax.axis_size("samp"))
    partner_count = counts[0]
    tiles = []
    for offset in range(WIN):
        if offset == 0:
            partner = scored
        else:
            partner = from_behind(scored, "var", -offset)
        tiles.append(
            lax.cond(
                offset < partner_count,
                lambda other: contract(scored, other),
                lambda other: jnp.zeros((width, width), jnp.float32),
                partner,
            )
        )
    stacked = jnp.stack(tiles)
    reduced = lax.psum_scatter(stacked, "samp", scatter_dimension=1, tiled=True)
    scaled = reduced / total_samples
    keep = jnp.arange(WIN, dtype=jnp.int32)[:, None, None] < partner_count
    result = jnp.where(keep, scaled, jnp.zeros_like(scaled)).astype(jnp.bfloat16)
    return result[None]


def solution(mesh):
    in_specs = (P("samp", ("region", "var")), P("samp", ("region", "var")), P(("region", "var")))
    out_specs = P(("region", "var"), None, "samp", None)
    return jax.shard_map(
        per_device, mesh=mesh, in_specs=in_specs, out_specs=out_specs, check_vma=False
    )
```

profile of v0, /device:TPU:0, one launch (start us, length us, event | category | flops | bytes accessed | tf_op | source)
XLA Modules:
  0.0 261.6 jit_solution(15636543799726126289)
XLA Ops:
  6.5 0.0 copy-start
  6.5 0.0 reduce-scatter.2.cloned.1.call-start
  6.5 4.0 %fusion.5 = (f32[1024]{0:T(1024)S(1)}, f32[1024]{0:T(1024)S(1)}, f32[1024]{0:T(1024)S(1)}) fusion(bf16[1024,1024]{1,0:T(8,128)(2,1)} %param.11, s32[1024,1024]{1,0:T(8,128)} %param.12), kind=kLoop, calls=%fused_computation.15 | loop fusion | flops 7336960 | bytes 6303744 | tf_op jit(solution)/shard_map/reduce_sum | solution.py:30
  10.6 3.6 %all-reduce = (f32[1024]{0:T(1024)S(1)}, f32[1024]{0:T(1024)S(1)}, f32[1024]{0:T(1024)S(1)}) all-reduce(f32[1024]{0:T(1024)S(1)} %get-tuple-element.41, f32[1024]{0:T(1024)S(1)} %get-tuple-element.42, f32[1024]{0:T(1024)S(1)} %get-tuple-element.40), channel_id=1, replica_groups=mesh['region'=2,'var'=8,'samp'=2] {'samp'}, use_global_device_ids=true, to_apply=%region_5.0 | all-reduce | flops 3072 | bytes 24576 | tf_op jit(solution)/shard_map/psum | solution.py:27
  14.2 0.0 copy-done
  14.2 4.4 %fusion.2 = bf16[1024,1024]{1,0:T(8,128)(2,1)} fusion(bf16[1024,1024]{1,0:T(8,128)(2,1)S(1)} %copy-done, s32[1024,1024]{1,0:T(8,128)} %param.12, f32[1024]{0:T(1024)S(1)} %get-tuple-element.47, f32[1024]{0:T(1024)S(1)} %get-tuple-element.46), kind=kLoop, calls=%fused_computation.11 | loop fusion | flops 6291456 | bytes 8396800 | tf_op jit(solution)/shard_map/convert_element_type | solution.py:39
  18.6 1.3 collective-permute-start.2
  19.9 1.3 collective-permute-start.1
  21.2 1.3 collective-permute-start
  23.1 6.6 %conditional.4 = (f32[1,1024,1024]{2,1,0:T(8,128)}) conditional(s32[]{:T(128)} %convert_element_type.27, () %tuple.37, bf16[1024,1024]{1,0:T(8,128)(2,1)} %fusion.2), branch_computations={%region_6.0_spmd, %region_7.0_spmd} | conditional | flops 2147483648 | bytes 6291464 | solution.py:50
  23.2 6.5 %convolution_bitcast_fusion = f32[1,1024,1024]{2,1,0:T(8,128)} fusion(bf16[1024,1024]{1,0:T(8,128)(2,1)} %param.1), kind=kOutput, calls=%fused_computation | convolution fusion | flops 2147483648 | bytes 6291456 | tf_op jit(solution)/shard_map/cond/branch_1_fun/dot_general | solution.py:19
  29.7 41.3 %collective-permute-done.2 = bf16[1024,1024]{1,0:T(8,128)(2,1)} collective-permute-done((bf16[1024,1024]{1,0:T(8,128)(2,1)}, bf16[1024,1024]{1,0:T(8,128)(2,1)}, u32[]{:S(2)}, u32[]{:S(2)}) %collective-permute-start.2) | collective-permute-done | bytes 2097184 | tf_op jit(solution)/shard_map/ppermute | solution.py:15
  71.0 6.6 %conditional.7 = (f32[1,1024,1024]{2,1,0:T(8,128)}) conditional(s32[]{:T(128)} %convert_element_type.33, () %tuple.42, (bf16[1024,1024]{1,0:T(8,128)(2,1)}, bf16[1024,1024]{1,0:T(8,128)(2,1)}) %tuple.43), branch_computations={%region_12.0_spmd, %region_13.0_spmd} | conditional | flops 2147483648 | bytes 8388616 | solution.py:50
  71.0 6.6 %convolution_bitcast_fusion.3 = f32[1,1024,1024]{2,1,0:T(8,128)} fusion(bf16[1024,1024]{1,0:T(8,128)(2,1)} %get-tuple-element.38, bf16[1024,1024]{1,0:T(8,128)(2,1)} %get-tuple-element.39), kind=kOutput, calls=%fused_computation.3 | convolution fusion | flops 2147483648 | bytes 8388608 | tf_op jit(solution)/shard_map/cond/branch_1_fun/dot_general | solution.py:19
  77.6 0.0 collective-permute-done.1
  77.6 6.6 %conditional.6 = (f32[1,1024,1024]{2,1,0:T(8,128)}) conditional(s32[]{:T(128)} %convert_element_type.32, () %tuple.40, (bf16[1024,1024]{1,0:T(8,128)(2,1)}, bf16[1024,1024]{1,0:T(8,128)(2,1)}) %tuple.41), branch_computations={%region_10.0_spmd, %region_11.0_spmd} | conditional | flops 2147483648 | bytes 8388616 | solution.py:50
  77.6 6.6 %convolution_bitcast_fusion.2 = f32[1,1024,1024]{2,1,0:T(8,128)} fusion(bf16[1024,1024]{1,0:T(8,128)(2,1)} %get-tuple-element.36, bf16[1024,1024]{1,0:T(8,128)(2,1)} %get-tuple-element.37), kind=kOutput, calls=%fused_computation.2 | convolution fusion | flops 2147483648 | bytes 8388608 | tf_op jit(solution)/shard_map/cond/branch_1_fun/dot_general | solution.py:19
  84.2 31.3 %collective-permute-done = bf16[1024,1024]{1,0:T(8,128)(2,1)S(1)} collective-permute-done((bf16[1024,1024]{1,0:T(8,128)(2,1)}, bf16[1024,1024]{1,0:T(8,128)(2,1)S(1)}, u32[]{:S(2)}, u32[]{:S(2)}) %collective-permute-start) | collective-permute-done | bytes 2097184 | tf_op jit(solution)/shard_map/ppermute | solution.py:15
  115.5 5.9 %conditional.5 = (f32[1,1024,1024]{2,1,0:T(8,128)}) conditional(s32[]{:T(128)} %convert_element_type.31, () %tuple.38, (bf16[1024,1024]{1,0:T(8,128)(2,1)}, bf16[1024,1024]{1,0:T(8,128)(2,1)S(1)}) %tuple.39), branch_computations={%region_8.0_spmd, %region_9.0_spmd} | conditional | flops 2147483648 | bytes 8388616 | solution.py:50
  115.5 5.9 %convolution_bitcast_fusion.1 = f32[1,1024,1024]{2,1,0:T(8,128)} fusion(bf16[1024,1024]{1,0:T(8,128)(2,1)} %get-tuple-element.34, bf16[1024,1024]{1,0:T(8,128)(2,1)S(1)} %get-tuple-element.35), kind=kOutput, calls=%fused_computation.1 | convolution fusion | flops 2147483648 | bytes 8388608 | tf_op jit(solution)/shard_map/cond/branch_1_fun/dot_general | solution.py:19
  121.4 11.7 %pad_maximum_fusion = f32[4,1024,1024]{2,1,0:T(8,128)} fusion(f32[1,1024,1024]{2,1,0:T(8,128)} %get-tuple-element.51, f32[1,1024,1024]{2,1,0:T(8,128)} %get-tuple-element.50, f32[1,1024,1024]{2,1,0:T(8,128)} %get-tuple-element.49, f32[1,1024,1024]{2,1,0:T(8,128)} %get-tuple-element.48), kind=kLoop, calls=%fused_computation.4 | loop fusion | flops 12582912 | bytes 33554432 | tf_op jit(solution)/shard_map/stack | solution.py:57
  133.1 0.0 reduce-scatter.2.cloned.1.call-update
  133.2 114.4 %reduce-scatter.2.cloned.1.call-done = f32[4,512,1024]{2,1,0:T(8,128)} async-done(((f32[4,1024,1024]{2,1,0:T(8,128)}), f32[4,512,1024]{2,1,0:T(8,128)}) %reduce-scatter.2.cloned.1.call-update) | async-done | bytes 8388624 | tf_op jit(solution)/shard_map/reduce_scatter | solution.py:58
  247.6 7.2 %fusion.4 = bf16[1,4,512,1024]{3,2,1,0:T(8,128)(2,1)} fusion(f32[4,512,1024]{2,1,0:T(8,128)} %reduce-scatter.2.cloned.1.call-done, pred[4]{0:T(512)(128)(4,1)S(1)} %iota_compare_fusion), kind=kLoop, calls=%fused_computation.13 | loop fusion | flops 6291456 | bytes 12582916 | tf_op jit(solution)/shard_map/broadcast_in_dim | solution.py:62
  (2 shorter events, 0.0 us)
Async XLA Ops:
  6.5 7.7 %copy-start = (bf16[1024,1024]{1,0:T(8,128)(2,1)S(1)}, bf16[1024,1024]{1,0:T(8,128)(2,1)}, u32[]{:S(2)}) copy-start(bf16[1024,1024]{1,0:T(8,128)(2,1)} %param.11) | copy-start | bytes 6291460
  6.5 241.1 %reduce-scatter.2.cloned.1.call-start = ((), (), s32[]{:S(2)}) async-start(), calls=%async_computation.1 | async-start | bytes 25165824 | tf_op jit(solution)/shard_map/reduce_scatter | solution.py:58
  18.6 52.4 %collective-permute-start.2 = (bf16[1024,1024]{1,0:T(8,128)(2,1)}, bf16[1024,1024]{1,0:T(8,128)(2,1)}, u32[]{:S(2)}, u32[]{:S(2)}) collective-permute-start(bf16[1024,1024]{1,0:T(8,128)(2,1)} %fusion.2), channel_id=1, source_target_pairs={{6,0},{8,2},{10,4},{12,6},{14,8},{7,1},{9,3},{11,5},{13,7},{15,9},... | collective-permute-start | bytes 6291464 | tf_op jit(solution)/shard_map/ppermute | solution.py:15
  19.9 57.7 %collective-permute-start.1 = (bf16[1024,1024]{1,0:T(8,128)(2,1)}, bf16[1024,1024]{1,0:T(8,128)(2,1)}, u32[]{:S(2)}, u32[]{:S(2)}) collective-permute-start(bf16[1024,1024]{1,0:T(8,128)(2,1)} %fusion.2), channel_id=1, source_target_pairs={{4,0},{6,2},{8,4},{10,6},{12,8},{14,10},{5,1},{7,3},{9,5},{11,7},{... | collective-permute-start | bytes 6291464 | tf_op jit(solution)/shard_map/ppermute | solution.py:15
  21.2 94.3 %collective-permute-start = (bf16[1024,1024]{1,0:T(8,128)(2,1)}, bf16[1024,1024]{1,0:T(8,128)(2,1)S(1)}, u32[]{:S(2)}, u32[]{:S(2)}) collective-permute-start(bf16[1024,1024]{1,0:T(8,128)(2,1)} %fusion.2), channel_id=1, source_target_pairs={{2,0},{4,2},{6,4},{8,6},{10,8},{12,10},{14,12},{3,1},{5,3},{7,5},{... | collective-permute-start | bytes 6291464 | tf_op jit(solution)/shard_map/ppermute | solution.py:15
Sparse Core Ops, SparseCore 0:
  133.3 114.2 reduce-scatter.1
where the time goes:
time: 262 us
  waiting for transfers between devices  187 us (71%)
  other arithmetic  27.3 us (10%)
  matrix products  25.7 us (10%)
  between operations  14.1 us (5%)
  starting transfers between devices  3.87 us (1%)
  blocking collectives  3.62 us (1%)
    reduce_scatter x1, waiting for transfers between devices, per_device(): reduced = lax.psum_scatter(stacked, 'samp', scatter_dimension=1, tiled=True)  114 us
    ppermute x3, waiting for transfers between devices, from_behind(): return lax.ppermute(shard, axis, pairs)  72.6 us
    dot_general x4, matrix products, contract(): lax.dot_general(left, right, (((0,), (0,)), ((), ())), preferred_element_...  25.7 us
    another operation x1, other arithmetic, per_device(): stacked = jnp.stack(tiles)  11.7 us
    broadcast_in_dim x1, other arithmetic, per_device(): return result[None]  7.17 us
  transfers between devices with their start and end apart: 4, of which 3 were waited for; matrix products, arithmetic and copies ran while one was open for 8% of the time, Pallas kernels for 0%

commit v1 on v0

v1 whole, which is shorter than its diff:
```python
import functools

import jax
import jax.numpy as jnp
from jax import lax
from jax.experimental import pallas as pl
from jax.experimental.pallas import tpu as pltpu
from jax.sharding import PartitionSpec as P

WIN = 4

epsilon = 1e-05

PIECES = 4
ROWS = 128


def kernel(
    n,
    total,
    d_ref,
    o_ref,
    out_ref,
    s0,
    s1,
    s2,
    t0,
    tm,
    r3s,
    r3r,
    stat_mine,
    stat_other,
    obuf,
    stat_sem,
    own_sem,
    down_sem,
    up_sem,
    y_sem,
    x1_sem,
    x2_sem,
    r3_sem,
    out_sem,
):
    b = lax.axis_index("var")
    c = lax.axis_index("samp")
    even = lax.rem(b, 2) == 0
    pair = b + 1 - 2 * lax.rem(b, 2)
    has_up = b + 2 < n
    has_down = b >= 2
    has_one = jnp.logical_or(even, has_up)
    core = {"samp": 1 - c}
    chunks, full, width = s0.shape
    half = chunks // 2
    local = full // 2
    steps = local // ROWS
    groups = ROWS // 8
    piece = full // PIECES
    tpiece = width // PIECES

    def remote(src, dst, sem, where):
        return pltpu.make_async_remote_copy(
            src_ref=src,
            dst_ref=dst,
            send_sem=sem.at[0],
            recv_sem=sem.at[1],
            device_id=where,
            device_id_type=pl.DeviceIdType.MESH,
        )

    barrier = pltpu.get_barrier_semaphore()
    pl.semaphore_signal(barrier, inc=1, device_id=core, device_id_type=pl.DeviceIdType.MESH)
    pl.semaphore_signal(
        barrier, inc=1, device_id={"var": pair}, device_id_type=pl.DeviceIdType.MESH
    )

    @pl.when(has_up)
    def _():
        pl.semaphore_signal(
            barrier, inc=1, device_id={"var": b + 2}, device_id_type=pl.DeviceIdType.MESH
        )

    @pl.when(has_down)
    def _():
        pl.semaphore_signal(
            barrier, inc=1, device_id={"var": b - 2}, device_id_type=pl.DeviceIdType.MESH
        )

    def column(ch):
        return pl.ds(ch * width, width)

    def load(ch, r):
        rows = pl.ds(pl.multiple_of(r * ROWS, ROWS), ROWS)
        present = o_ref[rows, column(ch)].astype(jnp.float32)
        return present, d_ref[rows, column(ch)].astype(jnp.float32)

    def fold(x):
        return jnp.sum(x.reshape(groups, 8, width), axis=0)

    stat_mine[...] = jnp.zeros_like(stat_mine)
    for ch in range(chunks):
        zero = jnp.zeros((8, width), jnp.float32)

        def first(r, carry):
            present, values = load(ch, r)
            return carry[0] + fold(present), carry[1] + fold(present * values)

        count8, sum8 = lax.fori_loop(0, steps, first, (zero, zero))
        count = jnp.sum(count8, axis=0, keepdims=True)
        summed = jnp.sum(sum8, axis=0, keepdims=True)
        mean = summed / jnp.maximum(count, 1.0)

        def second(r, carry):
            present, values = load(ch, r)
            off = present * (values - mean)
            return carry + fold(off * off)

        square = jnp.sum(lax.fori_loop(0, steps, second, zero), axis=0, keepdims=True)
        stat_mine[0:1, column(ch)] = count
        stat_mine[1:2, column(ch)] = summed
        stat_mine[2:3, column(ch)] = square

    pl.semaphore_wait(barrier, 2 + has_up.astype(jnp.int32) + has_down.astype(jnp.int32))

    stat_copy = remote(stat_mine, stat_other, stat_sem, core)
    stat_copy.start()
    stat_copy.wait()

    def own_copy(i, who):
        rows = pl.ds(pl.multiple_of(c * local, local), local)
        ref = s0.at[who * half + i, rows, :]
        return remote(ref, ref, own_sem.at[i], core)

    for order in range(2):
        who = (1 - c) if order == 0 else c
        for i in range(half):
            ch = who * half + i
            cols = pl.ds(pl.multiple_of(ch * width, width), width)
            n_a, n_b = stat_mine[0:1, cols], stat_other[0:1, cols]
            s_a, s_b = stat_mine[1:2, cols], stat_other[1:2, cols]
            count = jnp.maximum(n_a + n_b, 1.0)
            center = (s_a + s_b) / count
            gap_a = s_a / jnp.maximum(n_a, 1.0) - center
            gap_b = s_b / jnp.maximum(n_b, 1.0) - center
            square = (stat_mine[2:3, cols] + n_a * gap_a * gap_a) + (
                stat_other[2:3, cols] + n_b * gap_b * gap_b
            )
            scale = lax.rsqrt(square / count + epsilon)

            def third(r, carry):
                rows = pl.ds(pl.multiple_of(r * ROWS, ROWS), ROWS)
                present = o_ref[rows, cols].astype(jnp.float32)
                values = d_ref[rows, cols].astype(jnp.float32)
                out = (present * (values - center) * scale).astype(jnp.bfloat16)
                s0[ch, pl.ds(pl.multiple_of(c * local + r * ROWS, ROWS), ROWS), :] = out
                return carry

            lax.fori_loop(0, steps, third, 0)
            if order == 0:
                own_send(s0, remote, own_sem, ch, c, local, i, core).start()

    for i in range(half):
        ch = c * half + i
        own_recv(s0, remote, own_sem, ch, c, local, i, core).wait_recv()

        def down(p):
            ref = s0.at[ch, pl.ds(pl.multiple_of(p * piece, piece), piece), :]
            to = s2.at[ch, pl.ds(pl.multiple_of(p * piece, piece), piece), :]
            return remote(ref, to, down_sem.at[i * PIECES + p], {"var": b - 2})

        def sideways(p):
            ref = s0.at[ch, pl.ds(pl.multiple_of(p * piece, piece), piece), :]
            to = s1.at[ch, pl.ds(pl.multiple_of(p * piece, piece), piece), :]
            return remote(ref, to, y_sem.at[i * PIECES + p], {"var": pair})

        for p in range(PIECES):

            @pl.when(has_down)
            def _():
                down(p).start()

            @pl.when(jnp.logical_not(even))
            def _():
                sideways(p).start()

        for q in range(PIECES):
            t0[i * width : (i + 1) * width, q * piece : (q + 1) * piece] = s0[
                ch, q * piece : (q + 1) * piece, :
            ].T

        @pl.when(has_up)
        def _():
            for p in range(PIECES):
                rows = pl.ds(i * width + p * tpiece, tpiece)
                remote(
                    t0.at[rows, :], tm.at[rows, :], up_sem.at[i * PIECES + p], {"var": b + 2}
                ).start()

    rows_mine = pl.ds(pl.multiple_of(c * local, local), local)
    for i in range(half):
        ref = s0.at[c * half + i, rows_mine, :]
        remote(ref, ref, own_sem.at[half + i], core).start()

    def tile(k, rhs, ch):
        acc = jnp.dot(t0[...], rhs[ch], preferred_element_type=jnp.float32)
        cols = pl.ds(pl.multiple_of(ch * width, width), width)
        obuf[k, :, cols] = (acc * (1.0 / total)).astype(jnp.bfloat16)

    def own_tile(i, carry):
        tile(0, s0, c * half + i)
        return carry

    lax.fori_loop(0, half, own_tile, 0)
    for i in range(half):
        ref = s0.at[(1 - c) * half + i, pl.ds(pl.multiple_of((1 - c) * local, local), local), :]
        remote(ref, ref, own_sem.at[half + i], core).wait_recv()

    def other_tile(i, carry):
        tile(0, s0, (1 - c) * half + i)
        return carry

    lax.fori_loop(0, half, other_tile, 0)

    def store(k):
        return pltpu.make_async_copy(obuf.at[k], out_ref.at[k], out_sem.at[k])

    store(0).start()

    def part(ref, ch, p):
        return ref.at[ch, pl.ds(pl.multiple_of(p * piece, piece), piece), :]

    for i in range(half):
        mine = c * half + i
        theirs = (1 - c) * half + i

        def relay(p, carry):
            slot = i * PIECES + p

            @pl.when(has_up)
            def _():
                got = part(s2, mine, p)
                remote(got, got, down_sem.at[slot], {"var": b + 2}).wait_recv()
                remote(got, got, x2_sem.at[slot], core).start()

                @pl.when(even)
                def _():
                    remote(got, part(s1, mine, p), y_sem.at[slot], {"var": pair}).start()

            @pl.when(has_one)
            def _():
                got = part(s1, mine, p)
                remote(got, got, y_sem.at[slot], {"var": pair}).wait_recv()
                remote(got, got, x1_sem.at[slot], core).start()

            return carry

        lax.fori_loop(0, PIECES, relay, 0)

        @pl.when(has_one)
        def _():
            tile(1, s1, mine)

        @pl.when(has_up)
        def _():
            tile(2, s2, mine)

        if i == half - 1:

            @pl.when(has_down)
            def _():
                for slot in range(half * PIECES):
                    rows = pl.ds(slot * tpiece, tpiece)
                    remote(
                        tm.at[rows, :], tm.at[rows, :], up_sem.at[slot], {"var": b - 2}
                    ).wait_recv()

        def received(p, carry):
            slot = i * PIECES + p

            @pl.when(has_up)
            def _():
                got = part(s2, theirs, p)
                remote(got, got, x2_sem.at[slot], core).wait_recv()

            @pl.when(has_one)
            def _():
                got = part(s1, theirs, p)
                remote(got, got, x1_sem.at[slot], core).wait_recv()

            return carry

        lax.fori_loop(0, PIECES, received, 0)

        @pl.when(has_one)
        def _():
            tile(1, s1, theirs)

        @pl.when(has_up)
        def _():
            tile(2, s2, theirs)

    @pl.when(jnp.logical_and(has_down, has_one))
    def _():
        def behind(ch, carry):
            acc = jnp.dot(tm[...], s1[ch], preferred_element_type=jnp.float32)
            r3s[ch] = (acc * (1.0 / total)).astype(jnp.bfloat16)
            remote(r3s.at[ch], r3r.at[ch], r3_sem.at[ch], {"var": b - 2}).start()
            return carry

        lax.fori_loop(0, chunks, behind, 0)

    store(1).start()
    store(2).start()

    @pl.when(jnp.logical_and(has_up, jnp.logical_or(even, b + 4 < n)))
    def _():
        def arrive(ch, carry):
            remote(r3r.at[ch], r3r.at[ch], r3_sem.at[ch], {"var": b + 2}).wait_recv()
            obuf[3, :, pl.ds(pl.multiple_of(ch * width, width), width)] = r3r[ch]
            return carry

        lax.fori_loop(0, chunks, arrive, 0)

    store(3).start()

    for i in range(half):
        own_send(s0, remote, own_sem, (1 - c) * half + i, c, local, i, core).wait_send()
        ref = s0.at[c * half + i, rows_mine, :]
        remote(ref, ref, own_sem.at[half + i], core).wait_send()

    def drain(slot, carry):
        i = slot // PIECES
        p = lax.rem(slot, PIECES)
        ch = c * half + i
        rows = pl.ds(pl.multiple_of(slot * tpiece, tpiece), tpiece)

        @pl.when(has_down)
        def _():
            ref = part(s0, ch, p)
            remote(ref, ref, down_sem.at[slot], {"var": b - 2}).wait_send()

        @pl.when(jnp.logical_or(jnp.logical_not(even), has_up))
        def _():
            ref = part(s0, ch, p)
            remote(ref, ref, y_sem.at[slot], {"var": pair}).wait_send()

        @pl.when(has_up)
        def _():
            remote(t0.at[rows, :], t0.at[rows, :], up_sem.at[slot], {"var": b + 2}).wait_send()
            ref = part(s2, ch, p)
            remote(ref, ref, x2_sem.at[slot], core).wait_send()

        @pl.when(has_one)
        def _():
            ref = part(s1, ch, p)
            remote(ref, ref, x1_sem.at[slot], core).wait_send()

        return carry

    lax.fori_loop(0, half * PIECES, drain, 0)

    @pl.when(jnp.logical_and(has_down, has_one))
    def _():
        def sent(ch, carry):
            remote(r3s.at[ch], r3s.at[ch], r3_sem.at[ch], {"var": b - 2}).wait_send()
            return carry

        lax.fori_loop(0, chunks, sent, 0)

    for k in range(WIN):
        store(k).wait()


def own_send(s0, remote, own_sem, ch, c, local, i, core):
    ref = s0.at[ch, pl.ds(pl.multiple_of(c * local, local), local), :]
    return remote(ref, ref, own_sem.at[i], core)


def own_recv(s0, remote, own_sem, ch, c, local, i, core):
    ref = s0.at[ch, pl.ds(pl.multiple_of((1 - c) * local, local), local), :]
    return remote(ref, ref, own_sem.at[i], core)


def per_device(dosage, observed, counts):
    local, variants = dosage.shape
    n = lax.axis_size("var")
    full = local * lax.axis_size("samp")
    half = variants // 2
    width = 256
    chunks = variants // width
    slots = (chunks // 2) * PIECES
    dma = pltpu.SemaphoreType.DMA
    tiles = pl.pallas_call(
        functools.partial(kernel, n, float(full)),
        out_shape=jax.ShapeDtypeStruct((WIN, half, variants), jnp.bfloat16),
        in_specs=[pl.BlockSpec(memory_space=pltpu.VMEM)] * 2,
        out_specs=pl.BlockSpec(memory_space=pl.ANY),
        scratch_shapes=[
            pltpu.VMEM((chunks, full, width), jnp.bfloat16),
            pltpu.VMEM((chunks, full, width), jnp.bfloat16),
            pltpu.VMEM((chunks, full, width), jnp.bfloat16),
            pltpu.VMEM((half, full), jnp.bfloat16),
            pltpu.VMEM((half, full), jnp.bfloat16),
            pltpu.VMEM((chunks, half, width), jnp.bfloat16),
            pltpu.VMEM((chunks, half, width), jnp.bfloat16),
            pltpu.VMEM((8, variants), jnp.float32),
            pltpu.VMEM((8, variants), jnp.float32),
            pltpu.VMEM((WIN, half, variants), jnp.bfloat16),
            dma((2,)),
            dma((chunks, 2)),
            dma((slots, 2)),
            dma((slots, 2)),
            dma((slots, 2)),
            dma((slots, 2)),
            dma((slots, 2)),
            dma((chunks, 2)),
            dma((WIN,)),
        ],
        compiler_params=pltpu.CompilerParams(
            collective_id=0, has_side_effects=True, vmem_limit_bytes=50 * 1024 * 1024
        ),
    )(dosage, observed)
    keep = jnp.arange(WIN, dtype=jnp.int32)[:, None, None] < counts[0]
    return jnp.where(keep, tiles, jnp.zeros_like(tiles))[None]


def solution(mesh):
    in_specs = (P("samp", ("region", "var")), P("samp", ("region", "var")), P(("region", "var")))
    out_specs = P(("region", "var"), None, "samp", None)
    return jax.shard_map(
        per_device, mesh=mesh, in_specs=in_specs, out_specs=out_specs, check_vma=False
    )
```

time: 262 us -> 99 us (0.38)
  the two profiles are of different devices: /device:TPU:0 before, /device:TPU:14 now
where the time goes in v1:
time: 99 us; the launch traced here: 98.8 us
  Pallas kernels  92 us (93%)
  other arithmetic  4.55 us (5%)
  local copies, waits for them, and re-layouts  1.59 us (2%)
    pallas_call x1, Pallas kernels, per_device(): pl.pallas_call(functools.partial(kernel, n, float(full)), out_shape=jax.S...  92 us
    broadcast_in_dim x1, other arithmetic, per_device(): return jnp.where(keep, tiles, jnp.zeros_like(tiles))[None]  4.54 us

profile of v1, /device:TPU:14, one launch (start us, length us, event | category | flops | bytes accessed | tf_op | source)
XLA Modules:
  0.0 98.8 jit_solution(7134991472119424677)
XLA Ops:
  0.7 0.0 copy-start
  0.7 1.6 %copy-done = bf16[1024,1024]{1,0:T(8,128)(2,1)S(1)} copy-done((bf16[1024,1024]{1,0:T(8,128)(2,1)S(1)}, bf16[1024,1024]{1,0:T(8,128)(2,1)}, u32[]{:S(2)}) %copy-start) | copy-done | bytes 2097176
  2.3 92.0 %shard_map.37 = bf16[4,512,1024]{2,1,0:T(8,128)(2,1)} custom-call(bf16[1024,1024]{1,0:T(8,128)(2,1)S(1)} %copy-done, s32[1024,1024]{1,0:T(8,128)} %o_ref.1), custom_call_target="tpu_custom_call" | custom-call | tf_op jit(solution)/shard_map/pallas_call | solution.py:392
  94.3 4.5 %select_bitcast_fusion = bf16[1,4,512,1024]{3,2,1,0:T(8,128)(2,1)} fusion(bf16[4,512,1024]{2,1,0:T(8,128)(2,1)} %shard_map.37, pred[4]{0:T(512)(128)(4,1)S(1)} %iota_compare_fusion), kind=kLoop, calls=%fused_computation | loop fusion | flops 2097152 | bytes 8388612 | tf_op jit(solution)/shard_map/broadcast_in_dim | solution.py:423
  (1 shorter events, 0.0 us)
Async XLA Ops:
  0.7 1.6 %copy-start = (bf16[1024,1024]{1,0:T(8,128)(2,1)S(1)}, bf16[1024,1024]{1,0:T(8,128)(2,1)}, u32[]{:S(2)}) copy-start(bf16[1024,1024]{1,0:T(8,128)(2,1)} %d_ref.1) | copy-start | bytes 6291460

commit v2 on v1

v2 whole, which is shorter than its diff:
```python
import functools

import jax
import jax.numpy as jnp
from jax import lax
from jax.experimental import pallas as pl
from jax.experimental.pallas import tpu as pltpu
from jax.sharding import PartitionSpec as P

WIN = 4

epsilon = 1e-05

PIECES = 4
ROWS = 128
INPUT = pltpu.HBM
VMEM_LIMIT = 38 * 1024 * 1024


def kernel(
    n,
    total,
    d_hbm,
    o_hbm,
    out_ref,
    d_ref,
    o_ref,
    s0,
    s1,
    s2,
    t0,
    tm,
    r3s,
    r3r,
    stat_mine,
    stat_other,
    obuf,
    in_sem,
    stat_sem,
    own_sem,
    down_sem,
    up_sem,
    y_sem,
    x1_sem,
    x2_sem,
    r3_sem,
    out_sem,
    out3_sem,
):
    b = lax.axis_index("var")
    c = lax.axis_index("samp")
    even = lax.rem(b, 2) == 0
    odd = jnp.logical_not(even)
    pair = b + 1 - 2 * lax.rem(b, 2)
    has_up = b + 2 < n
    has_down = b >= 2
    has_one = jnp.logical_or(even, has_up)
    sends_back = jnp.logical_and(has_down, has_one)
    gets_back = jnp.logical_and(has_up, jnp.logical_or(even, b + 4 < n))
    core = {"samp": 1 - c}
    below, above, beside = {"var": b - 2}, {"var": b + 2}, {"var": pair}
    chunks, full, width = s0.shape
    half = chunks // 2
    local = full // 2
    steps = local // ROWS
    groups = ROWS // 8
    piece = full // PIECES
    tpiece = width // PIECES
    mesh_id = pl.DeviceIdType.MESH

    def load(ch):
        cols = pl.ds(pl.multiple_of(ch * width, width), width)
        return (
            pltpu.make_async_copy(o_hbm.at[:, cols], o_ref.at[ch], in_sem.at[ch, 0]),
            pltpu.make_async_copy(d_hbm.at[:, cols], d_ref.at[ch], in_sem.at[ch, 1]),
        )

    for i in range(half):
        for who in range(2):
            for copy in load(who * half + i):
                copy.start()

    def remote(src, dst, sem, where):
        return pltpu.make_async_remote_copy(
            src_ref=src,
            dst_ref=dst,
            send_sem=sem.at[0],
            recv_sem=sem.at[1],
            device_id=where,
            device_id_type=mesh_id,
        )

    barrier = pltpu.get_barrier_semaphore()
    pl.semaphore_signal(barrier, inc=1, device_id=core, device_id_type=mesh_id)
    pl.semaphore_signal(barrier, inc=1, device_id=beside, device_id_type=mesh_id)

    @pl.when(has_up)
    def _():
        pl.semaphore_signal(barrier, inc=1, device_id=above, device_id_type=mesh_id)

    @pl.when(has_down)
    def _():
        pl.semaphore_signal(barrier, inc=1, device_id=below, device_id_type=mesh_id)

    def fold(x):
        return jnp.sum(x.reshape(groups, 8, width), axis=0)

    def block_rows(r):
        return pl.ds(pl.multiple_of(r * ROWS, ROWS), ROWS)

    def read(ch, r):
        present = o_ref[ch, block_rows(r), :].astype(jnp.float32)
        return present, d_ref[ch, block_rows(r), :].astype(jnp.float32)

    stat_mine[...] = jnp.zeros_like(stat_mine)

    def sums(i):
        for who in range(2):
            ch = who * half + i
            for copy in load(ch):
                copy.wait()
            zero = jnp.zeros((8, width), jnp.float32)

            def first(r, carry):
                present, values = read(ch, r)
                return carry[0] + fold(present), carry[1] + fold(present * values)

            count8, sum8 = lax.fori_loop(0, steps, first, (zero, zero))
            count = jnp.sum(count8, axis=0, keepdims=True)
            summed = jnp.sum(sum8, axis=0, keepdims=True)
            mean = summed / jnp.maximum(count, 1.0)

            def second(r, carry):
                present, values = read(ch, r)
                off = present * (values - mean)
                return carry + fold(off * off)

            square = jnp.sum(lax.fori_loop(0, steps, second, zero), axis=0, keepdims=True)
            cols = slice(who * width, (who + 1) * width)
            stat_mine[i, 0:1, cols] = count
            stat_mine[i, 1:2, cols] = summed
            stat_mine[i, 2:3, cols] = square

    def stat_copy(i):
        return remote(stat_mine.at[i], stat_other.at[i], stat_sem.at[i], core)

    sums(0)
    pl.semaphore_wait(barrier, 2 + has_up.astype(jnp.int32) + has_down.astype(jnp.int32))
    stat_copy(0).start()

    def samples_of(who, ch):
        return s0.at[ch, pl.ds(pl.multiple_of(who * local, local), local), :]

    def score(who, i):
        ch = who * half + i
        cols = pl.ds(pl.multiple_of(who * width, width), width)
        n_a, n_b = stat_mine[i, 0:1, cols], stat_other[i, 0:1, cols]
        s_a, s_b = stat_mine[i, 1:2, cols], stat_other[i, 1:2, cols]
        count = jnp.maximum(n_a + n_b, 1.0)
        center = (s_a + s_b) / count
        gap_a = s_a / jnp.maximum(n_a, 1.0) - center
        gap_b = s_b / jnp.maximum(n_b, 1.0) - center
        square = (stat_mine[i, 2:3, cols] + n_a * gap_a * gap_a) + (
            stat_other[i, 2:3, cols] + n_b * gap_b * gap_b
        )
        scale = lax.rsqrt(square / count + epsilon)

        def third(r, carry):
            present, values = read(ch, r)
            out = (present * (values - center) * scale).astype(jnp.bfloat16)
            s0[ch, pl.ds(pl.multiple_of(c * local + r * ROWS, ROWS), ROWS), :] = out
            return carry

        lax.fori_loop(0, steps, third, 0)

    def part(ref, ch, p):
        at = lax.rem(p + c * (PIECES // 2), PIECES)
        return ref.at[ch, pl.ds(pl.multiple_of(at * piece, piece), piece), :]

    def send_pieces(i, pieces):
        ch = c * half + i
        for p in pieces:
            slot = i * PIECES + p

            @pl.when(has_down)
            def _():
                remote(part(s0, ch, p), part(s2, ch, p), down_sem.at[slot], below).start()

            @pl.when(odd)
            def _():
                remote(part(s0, ch, p), part(s1, ch, p), y_sem.at[slot], beside).start()

    def own_out(i):
        ref = samples_of(c, (1 - c) * half + i)
        return remote(ref, ref, own_sem.at[i], core)

    def own_in(i):
        ref = samples_of(1 - c, c * half + i)
        return remote(ref, ref, own_sem.at[i], core)

    def second_out(i):
        ref = samples_of(c, c * half + i)
        return remote(ref, ref, own_sem.at[half + i], core)

    def second_in(i):
        ref = samples_of(1 - c, (1 - c) * half + i)
        return remote(ref, ref, own_sem.at[half + i], core)

    for i in range(half):
        later = i + 1 if i + 1 < half else None
        stat_copy(i).wait()
        score(c, i)
        if i == 0:
            send_pieces(i, range(PIECES // 2))
        score(1 - c, i)
        own_out(i).start()
        if later is not None:
            sums(later)
            stat_copy(later).start()
        own_in(i).wait_recv()
        if i == 0:
            send_pieces(i, range(PIECES // 2, PIECES))
        else:
            send_pieces(i, range(PIECES))
        ch = c * half + i
        for q in range(PIECES):
            t0[i * width : (i + 1) * width, q * piece : (q + 1) * piece] = s0[
                ch, q * piece : (q + 1) * piece, :
            ].T

        @pl.when(has_up)
        def _():
            for p in range(PIECES):
                rows = pl.ds(i * width + p * tpiece, tpiece)
                slot = i * PIECES + p
                remote(t0.at[rows, :], tm.at[rows, :], up_sem.at[slot], above).start()

    for i in range(half):
        second_out(i).start()

    def tile(k, rhs, ch):
        acc = jnp.dot(t0[...], rhs[ch], preferred_element_type=jnp.float32)
        cols = pl.ds(pl.multiple_of(ch * width, width), width)
        obuf[k, :, cols] = (acc * (1.0 / total)).astype(jnp.bfloat16)

    def own_tile(i, carry):
        tile(0, s0, c * half + i)
        return carry

    lax.fori_loop(0, half, own_tile, 0)
    for i in range(half):
        second_in(i).wait_recv()

    def other_tile(i, carry):
        tile(0, s0, (1 - c) * half + i)
        return carry

    lax.fori_loop(0, half, other_tile, 0)

    def store(k):
        return pltpu.make_async_copy(obuf.at[k], out_ref.at[k], out_sem.at[k])

    store(0).start()

    def relay_two(i, p):
        slot = i * PIECES + p

        @pl.when(has_up)
        def _():
            got = part(s2, c * half + i, p)
            remote(got, got, down_sem.at[slot], above).wait_recv()

            @pl.when(even)
            def _():
                remote(got, part(s1, c * half + i, p), y_sem.at[slot], beside).start()

            remote(got, got, x2_sem.at[slot], core).start()

    def relay_one(i, p):
        slot = i * PIECES + p

        @pl.when(has_one)
        def _():
            got = part(s1, c * half + i, p)
            remote(got, got, y_sem.at[slot], beside).wait_recv()
            remote(got, got, x1_sem.at[slot], core).start()

    def received(ref, sem, i):
        def one(p, carry):
            got = part(ref, (1 - c) * half + i, p)
            remote(got, got, sem.at[i * PIECES + p], core).wait_recv()
            return carry

        lax.fori_loop(0, PIECES, one, 0)

    def turned(i):
        @pl.when(has_down)
        def _():
            for p in range(PIECES):
                rows = pl.ds(i * width + p * tpiece, tpiece)
                ref = tm.at[rows, :]
                remote(ref, ref, up_sem.at[i * PIECES + p], below).wait_recv()

    def back_copy(h, ch, where):
        return remote(r3s.at[h, ch], r3r.at[h, ch], r3_sem.at[h, ch], where)

    def behind(h, ch):
        acc = jnp.dot(
            tm[h * width : (h + 1) * width, :], s1[ch], preferred_element_type=jnp.float32
        )
        r3s[h, ch] = (acc * (1.0 / total)).astype(jnp.bfloat16)
        back_copy(h, ch, below).start()

    for i in range(half):
        mine = c * half + i
        theirs = (1 - c) * half + i
        last = i == half - 1
        for p in range(PIECES):
            relay_two(i, p)
            if last and p == PIECES - 1:
                turned(i)

                @pl.when(sends_back)
                def _():
                    for j in range(i):
                        behind(i, c * half + j)
                        behind(i, (1 - c) * half + j)

            relay_one(i, p)
        if not last:
            turned(i)

        @pl.when(sends_back)
        def _():
            for h in range(i + 1):
                behind(h, mine)

        @pl.when(has_one)
        def _():
            received(s1, x1_sem, i)

        @pl.when(sends_back)
        def _():
            for h in range(i + 1):
                behind(h, theirs)

        @pl.when(has_one)
        def _():
            tile(1, s1, mine)
            tile(1, s1, theirs)

        @pl.when(has_up)
        def _():
            tile(2, s2, mine)
            received(s2, x2_sem, i)
            tile(2, s2, theirs)

    store(1).start()
    store(2).start()

    def back_store(h, ch):
        rows = pl.ds(h * width, width)
        cols = pl.ds(pl.multiple_of(ch * width, width), width)
        return pltpu.make_async_copy(
            r3r.at[h, ch], out_ref.at[WIN - 1, rows, cols], out3_sem.at[h, ch]
        )

    parts = []
    for i in range(half):
        for j in range(i):
            parts += [(i, 0, j), (i, 1, j)]
        for side in range(2):
            for h in range(i + 1):
                parts.append((h, side, i))

    @pl.when(gets_back)
    def _():
        for h, side, j in parts:
            ch = (c if side == 0 else 1 - c) * half + j
            back_copy(h, ch, above).wait_recv()
            back_store(h, ch).start()
        for h, side, j in parts:
            back_store(h, (c if side == 0 else 1 - c) * half + j).wait()

    for i in range(half):
        own_out(i).wait_send()
        second_out(i).wait_send()

    def drain(slot, carry):
        i = slot // PIECES
        p = lax.rem(slot, PIECES)
        ch = c * half + i
        rows = pl.ds(pl.multiple_of(slot * tpiece, tpiece), tpiece)

        @pl.when(has_down)
        def _():
            ref = part(s0, ch, p)
            remote(ref, ref, down_sem.at[slot], below).wait_send()

        @pl.when(jnp.logical_or(odd, has_up))
        def _():
            ref = part(s0, ch, p)
            remote(ref, ref, y_sem.at[slot], beside).wait_send()

        @pl.when(has_up)
        def _():
            remote(t0.at[rows, :], t0.at[rows, :], up_sem.at[slot], above).wait_send()
            ref = part(s2, ch, p)
            remote(ref, ref, x2_sem.at[slot], core).wait_send()

        @pl.when(has_one)
        def _():
            ref = part(s1, ch, p)
            remote(ref, ref, x1_sem.at[slot], core).wait_send()

        return carry

    lax.fori_loop(0, half * PIECES, drain, 0)

    @pl.when(sends_back)
    def _():
        for h in range(half):
            for ch in range(chunks):
                back_copy(h, ch, below).wait_send()

    for k in range(WIN - 1):
        store(k).wait()


def per_device(dosage, observed, counts):
    local, variants = dosage.shape
    n = lax.axis_size("var")
    full = local * lax.axis_size("samp")
    half = variants // 2
    width = 256
    chunks = variants // width
    slots = (chunks // 2) * PIECES
    dma = pltpu.SemaphoreType.DMA
    tiles = pl.pallas_call(
        functools.partial(kernel, n, float(full)),
        out_shape=jax.ShapeDtypeStruct((WIN, half, variants), jnp.bfloat16),
        in_specs=[pl.BlockSpec(memory_space=INPUT)] * 2,
        out_specs=pl.BlockSpec(memory_space=pl.ANY),
        scratch_shapes=[
            pltpu.VMEM((chunks, local, width), dosage.dtype),
            pltpu.VMEM((chunks, local, width), observed.dtype),
            pltpu.VMEM((chunks, full, width), jnp.bfloat16),
            pltpu.VMEM((chunks, full, width), jnp.bfloat16),
            pltpu.VMEM((chunks, full, width), jnp.bfloat16),
            pltpu.VMEM((half, full), jnp.bfloat16),
            pltpu.VMEM((half, full), jnp.bfloat16),
            pltpu.VMEM((chunks // 2, chunks, width, width), jnp.bfloat16),
            pltpu.VMEM((chunks // 2, chunks, width, width), jnp.bfloat16),
            pltpu.VMEM((chunks // 2, 8, 2 * width), jnp.float32),
            pltpu.VMEM((chunks // 2, 8, 2 * width), jnp.float32),
            pltpu.VMEM((WIN - 1, half, variants), jnp.bfloat16),
            dma((chunks, 2)),
            dma((chunks // 2, 2)),
            dma((chunks, 2)),
            dma((slots, 2)),
            dma((slots, 2)),
            dma((slots, 2)),
            dma((slots, 2)),
            dma((slots, 2)),
            dma((chunks // 2, chunks, 2)),
            dma((WIN - 1,)),
            dma((chunks // 2, chunks)),
        ],
        compiler_params=pltpu.CompilerParams(
            collective_id=0, has_side_effects=True, vmem_limit_bytes=VMEM_LIMIT
        ),
    )(pltpu.with_memory_space_constraint(dosage, pltpu.HBM), pltpu.with_memory_space_constraint(observed, pltpu.HBM))
    keep = jnp.arange(WIN, dtype=jnp.int32)[:, None, None] < counts[0]
    return jnp.where(keep, tiles, jnp.zeros_like(tiles))[None]


def solution(mesh):
    in_specs = (P("samp", ("region", "var")), P("samp", ("region", "var")), P(("region", "var")))
    out_specs = P(("region", "var"), None, "samp", None)
    return jax.shard_map(
        per_device, mesh=mesh, in_specs=in_specs, out_specs=out_specs, check_vma=False
    )
```

time: 99 us -> 79.6 us (0.80)
  the two profiles are of different devices: /device:TPU:14 before, /device:TPU:0 now
where the time goes in v2:
time: 79.6 us; the launch traced here: 79.4 us
  Pallas kernels  76.4 us (96%)
  other arithmetic  2.36 us (3%)
    pallas_call x1, Pallas kernels, per_device(): pl.pallas_call(functools.partial(kernel, n, float(full)), out_shape=jax.S...  76.4 us
    broadcast_in_dim x1, other arithmetic, per_device(): return jnp.where(keep, tiles, jnp.zeros_like(tiles))[None]  2.36 us

profile of v2, /device:TPU:0, one launch (start us, length us, event | category | flops | bytes accessed | tf_op | source)
XLA Modules:
  0.0 79.4 jit_solution(5176449686535322310)
XLA Ops:
  0.7 76.4 %shard_map.37 = bf16[4,512,1024]{2,1,0:T(8,128)(2,1)S(1)} custom-call(bf16[1024,1024]{1,0:T(8,128)(2,1)} %d_hbm.1, s32[1024,1024]{1,0:T(8,128)} %o_hbm.1), custom_call_target="tpu_custom_call" | custom-call | tf_op jit(solution)/shard_map/pallas_call | solution.py:439
  77.1 2.4 %select_bitcast_fusion = bf16[1,4,512,1024]{3,2,1,0:T(8,128)(2,1)} fusion(bf16[4,512,1024]{2,1,0:T(8,128)(2,1)S(1)} %shard_map.37, pred[4]{0:T(512)(128)(4,1)S(1)} %iota_compare_fusion), kind=kLoop, calls=%fused_computation | loop fusion | flops 2097152 | bytes 8388612 | tf_op jit(solution)/shard_map/broadcast_in_dim | solution.py:474
  (1 shorter events, 0.0 us)
